TPU v7x, 32 devices: a whole 2x2x4 slice. The times are simulated.
32 devices in a mesh: dp: 4 (over y, x), mp: 8 (over z, core).
Axes of the slice: x: 2, y: 2, z: 4, core: 2. Of those that a mesh axis runs over, the one named last changes fastest.
Arguments:
- tokens: bfloat16 [512, 6144], P(('dp', 'mp')), may hold values from -6 to 6
- norm_gain: float32 [6144], replicated, may hold values from 0.5 to 1.5
- up_weight: bfloat16 [6144, 16384], P(None, 'mp'), may hold values from -0.078125 to 0.078125
- down_weight: bfloat16 [16384, 6144], P('mp'), may hold values from -0.046875 to 0.046875
- out_grad: bfloat16 [512, 6144], P(('dp', 'mp')), may hold values from -6 to 6
Outputs:
- input_grad: bfloat16 [512, 6144], P(('dp', 'mp'))
- up_grad: bfloat16 [6144, 16384], P('dp', 'mp')
- down_grad: bfloat16 [16384, 6144], P('mp', 'dp')
- gain_grad: float32 [6144], replicated
All inputs are finite; a program needn't handle non-finite values.
Results may differ from a plain program's by a relative error of at most 0.018.
Values may be sent and summed in bfloat16 or wider, within the bound.
No kernel may reach another device: no remote copies, remote signals or barrier semaphores. Data moves between devices by JAX's collectives and lax.ppermute only.
A program may use at most 192 MiB of HBM per device.

v0:
```python
import math
import jax
import jax.numpy as jnp
from jax import lax
from jax.sharding import PartitionSpec as P


def gelu_value(preact):
    return 0.5 * preact * (1.0 + lax.erf(preact * 0.7071067811865476))


def gelu_slope(preact):
    return (
        0.5 * (1.0 + lax.erf(preact * 0.7071067811865476))
        + preact * jnp.exp(-0.5 * preact * preact) * 0.3989422804014327
    )


def per_device(tokens, norm_gain, up_weight, down_weight, out_grad):
    values = tokens.astype(jnp.float32)
    centered = values - jnp.mean(values, axis=1, keepdims=True)
    inv_std = lax.rsqrt(jnp.mean(centered * centered, axis=1, keepdims=True) + 1e-06)
    x_hat = centered * inv_std
    normed = (x_hat * norm_gain).astype(jnp.bfloat16)
    normed_all, cotan_all = (
        lax.all_gather(normed, "mp", axis=0, tiled=True),
        lax.all_gather(out_grad, "mp", axis=0, tiled=True),
    )
    preact = jnp.dot(normed_all, up_weight, preferred_element_type=jnp.float32)
    hidden = gelu_value(preact).astype(jnp.bfloat16)
    hid_grad = lax.dot_general(
        cotan_all, down_weight, (((1,), (1,)), ((), ())), preferred_element_type=jnp.float32
    )
    pre_grad = (hid_grad * gelu_slope(preact)).astype(jnp.bfloat16)
    norm_grad = lax.psum_scatter(
        lax.dot_general(
            pre_grad, up_weight, (((1,), (1,)), ((), ())), preferred_element_type=jnp.float32
        ),
        "mp",
        scatter_dimension=0,
        tiled=True,
    )
    replicas = lax.axis_size("dp")
    group = normed_all.shape[0]
    factor = 1.0 / math.sqrt(group * replicas)
    gain_grad = lax.psum(jnp.sum(norm_grad * x_hat, axis=0), ("dp", "mp")) * factor
    scaled = norm_gain * norm_grad
    input_grad = (
        scaled
        - jnp.mean(scaled, axis=1, keepdims=True)
        - x_hat * jnp.mean(scaled * x_hat, axis=1, keepdims=True)
    ) * inv_std
    normed_cols, cotan_cols = (
        lax.all_to_all(normed_all, "dp", split_axis=1, concat_axis=0, tiled=True),
        lax.all_to_all(cotan_all, "dp", split_axis=1, concat_axis=0, tiled=True),
    )
    hidden_all, pre_all = (
        lax.all_gather(hidden, "dp", axis=0, tiled=True),
        lax.all_gather(pre_grad, "dp", axis=0, tiled=True),
    )

    def stacked(array):
        return array.reshape(replicas, group, array.shape[1])

    up_parts = jnp.einsum(
        "rtk,rtf->rkf", stacked(normed_cols), stacked(pre_all), preferred_element_type=jnp.float32
    )
    down_parts = jnp.einsum(
        "rtf,rtk->rfk", stacked(hidden_all), stacked(cotan_cols), preferred_element_type=jnp.float32
    )
    up_total = jnp.sum(up_parts.astype(jnp.bfloat16).astype(jnp.float32), axis=0)
    down_total = jnp.sum(down_parts.astype(jnp.bfloat16).astype(jnp.float32), axis=0)
    up_grad = (up_total * factor).astype(jnp.bfloat16)
    down_grad = (down_total * factor).astype(jnp.bfloat16)
    return (input_grad.astype(jnp.bfloat16), up_grad, down_grad, gain_grad)


def solution(mesh):
    placed = (P(("dp", "mp"), None), P(), P(None, "mp"), P("mp", None), P(("dp", "mp"), None))
    return jax.shard_map(
        per_device,
        mesh=mesh,
        in_specs=placed,
        out_specs=(P(("dp", "mp"), None), P("dp", "mp"), P("mp", "dp"), P()),
        check_vma=False,
    )
```

profile of v0, /device:TPU:10, one launch (start us, length us, event | category | flops | bytes accessed | tf_op | source)
XLA Modules:
  0.0 251.2 jit_solution(14012743861452806159)
XLA Ops:
  7.2 0.0 all-gather.7.cloned.1.call-start
  7.2 1.1 convert_reduce_fusion.2
  8.3 1.2 fusion.19
  9.5 1.7 fusion.13
  11.2 0.0 all-gather.7.cloned.1.call-update
  11.2 0.0 all-gather.5.cloned.1.call-start
  11.3 0.7 all-gather.5.cloned.1.call-update
  12.0 0.0 all-gather.11.cloned.1.call-start
  12.0 25.4 %all-gather.7.cloned.1.call-done = bf16[128,6144]{1,0:T(8,128)(2,1)} async-done(((bf16[16,6144]{1,0:T(8,128)(2,1)}), bf16[128,6144]{1,0:T(8,128)(2,1)}) %all-gather.7.cloned.1.call-update) | async-done | bytes 1572880 | tf_op jit(solution)/shard_map/all_gather | solution.py:26
  37.5 13.1 %multiply_convert_fusion.2 = (bf16[128,2048]{1,0:T(8,128)(2,1)}, f32[128,2048]{1,0:T(8,128)S(1)}) fusion(bf16[128,6144]{1,0:T(8,128)(2,1)} %all-gather.7.cloned.1.call-done, bf16[6144,2048]{1,0:T(8,128)(2,1)} %param.7), kind=kOutput, calls=%fused_computation.15 | convolution fusion | flops 3222536192 | bytes 28311552 | tf_op jit(solution)/shard_map/dot_general | solution.py:29
  50.6 0.0 all-gather.11.cloned.1.call-update
  50.6 0.0 all-gather.9.cloned.1.call-start
  50.6 12.9 %all-gather.5.cloned.1.call-done = bf16[128,6144]{1,0:T(8,128)(2,1)} async-done(((bf16[16,6144]{1,0:T(8,128)(2,1)}), bf16[128,6144]{1,0:T(8,128)(2,1)}) %all-gather.5.cloned.1.call-update) | async-done | bytes 1572880 | tf_op jit(solution)/shard_map/all_gather | solution.py:27
  63.5 14.3 %fusion = bf16[128,2048]{1,0:T(8,128)(2,1)} fusion(bf16[128,6144]{1,0:T(8,128)(2,1)} %all-gather.5.cloned.1.call-done, bf16[2048,6144]{1,0:T(8,128)(2,1)} %param.8, f32[128,2048]{1,0:T(8,128)S(1)} %get-tuple-element.8), kind=kOutput, calls=%fused_computation.7 | convolution fusion | flops 3223846912 | bytes 28311552 | tf_op jit(solution)/shard_map/dot_general | solution.py:31
  77.8 0.0 all-gather.9.cloned.1.call-update
  77.8 0.0 copy-start
  77.9 0.0 reduce-scatter.2.cloned.1.call-start
  77.9 14.4 %fusion.20 = f32[128,6144]{1,0:T(8,128)} fusion(bf16[128,2048]{1,0:T(8,128)(2,1)} %fusion, bf16[6144,2048]{1,0:T(8,128)(2,1)} %param.7), kind=kOutput, calls=%fused_computation.38 | convolution fusion | flops 3221225472 | bytes 28835840 | tf_op jit(solution)/shard_map/dot_general | solution.py:36
  92.4 0.0 copy-start.1
  92.4 0.0 reduce-scatter.2.cloned.1.call-update
  92.4 0.0 copy-done
  92.4 1.6 copy.16
  94.0 2.6 %copy.17 = bf16[128,4,1536]{2,0,1:T(8,128)(2,1)} copy(bf16[128,4,1536]{0,2,1:T(8,128)(2,1)} %bitcast.18) | data formatting | bytes 3145728 | tf_op jit(solution)/shard_map/all_to_all | solution.py:55
  96.5 4.2 %all-to-all-start.1 = ((bf16[128,4,1536]{2,0,1:T(8,128)(2,1)}), bf16[128,4,1536]{2,0,1:T(8,128)(2,1)S(1)}, u32[]{:S(2)}, u32[]{:S(2)}) async-start(bf16[128,4,1536]{2,0,1:T(8,128)(2,1)} %copy.17), calls=%async_computation.2 | async-start | bytes 3145728 | tf_op jit(solution)/shard_map/all_to_all | solution.py:55
  100.7 0.0 copy-done.1
  100.7 1.6 copy.20
  102.3 23.3 %all-to-all-done.1 = bf16[128,4,1536]{2,0,1:T(8,128)(2,1)S(1)} async-done(((bf16[128,4,1536]{2,0,1:T(8,128)(2,1)}), bf16[128,4,1536]{2,0,1:T(8,128)(2,1)S(1)}, u32[]{:S(2)}, u32[]{:S(2)}) %all-to-all-start.1) | async-done | bytes 1572896 | tf_op jit(solution)/shard_map/all_to_all | solution.py:55
  125.6 4.1 %all-to-all-start = ((bf16[128,4,1536]{0,2,1:T(8,128)(2,1)}), bf16[128,4,1536]{0,2,1:T(8,128)(2,1)S(1)}, u32[]{:S(2)}, u32[]{:S(2)}) async-start(bf16[128,4,1536]{0,2,1:T(8,128)(2,1)} %bitcast), calls=%async_computation.1 | async-start | bytes 3145728 | tf_op jit(solution)/shard_map/all_to_all | solution.py:54
  129.7 0.0 all-gather.11.cloned.1.call-done
  129.7 14.2 %convert_reduce_fusion = f32[2048,1536]{1,0:T(8,128)} fusion(bf16[4,128,2048]{2,1,0:T(8,128)(2,1)} %bitcast.19, bf16[128,4,1536]{2,0,1:T(8,128)(2,1)S(1)} %all-to-all-done.1), kind=kOutput, calls=%fused_computation | convolution fusion | flops 3255828480 | bytes 16252928 | tf_op jit(solution)/shard_map/rtf,rtk->rfk/dot_general | solution.py:68
  143.9 15.4 %all-to-all-done = bf16[128,4,1536]{0,2,1:T(8,128)(2,1)S(1)} async-done(((bf16[128,4,1536]{0,2,1:T(8,128)(2,1)}), bf16[128,4,1536]{0,2,1:T(8,128)(2,1)S(1)}, u32[]{:S(2)}, u32[]{:S(2)}) %all-to-all-start) | async-done | bytes 1572896 | tf_op jit(solution)/shard_map/all_to_all | solution.py:54
  159.3 0.0 all-gather.9.cloned.1.call-done
  159.3 14.0 %convert_reduce_fusion.1 = f32[1536,2048]{1,0:T(8,128)} fusion(bf16[4,128,2048]{2,1,0:T(8,128)(2,1)} %bitcast.20, bf16[128,4,1536]{0,2,1:T(8,128)(2,1)S(1)} %all-to-all-done), kind=kOutput, calls=%fused_computation.1 | convolution fusion | flops 3255828480 | bytes 16252928 | tf_op jit(solution)/shard_map/rtk,rtf->rkf/dot_general | solution.py:65
  173.3 9.2 %multiply_convert_fusion = bf16[2048,1536]{1,0:T(8,128)(2,1)} fusion(f32[2048,1536]{1,0:T(8,128)} %convert_reduce_fusion), kind=kLoop, calls=%fused_computation.4 | loop fusion | flops 6291456 | bytes 18874368 | tf_op jit(solution)/shard_map/convert_element_type | solution.py:74
  182.4 0.0 copy-start.2
  182.4 0.0 copy-start.3
  182.4 9.3 %multiply_convert_fusion.1 = bf16[1536,2048]{1,0:T(8,128)(2,1)} fusion(f32[1536,2048]{1,0:T(8,128)} %convert_reduce_fusion.1), kind=kLoop, calls=%fused_computation.5 | loop fusion | flops 6291456 | bytes 18874368 | tf_op jit(solution)/shard_map/convert_element_type | solution.py:73
  191.7 4.7 %reduce-scatter.2.cloned.1.call-done = f32[16,6144]{1,0:T(8,128)} async-done(((f32[128,6144]{1,0:T(8,128)}), f32[16,6144]{1,0:T(8,128)}) %reduce-scatter.2.cloned.1.call-update) | async-done | bytes 393232 | tf_op jit(solution)/shard_map/reduce_scatter | solution.py:35
  196.5 0.0 copy-done.2
  196.5 0.0 copy-done.3
  196.5 1.3 fusion.18
  197.8 44.4 %psum.7 = f32[6144]{0:T(1024)S(1)} all-reduce(f32[6144]{0:T(1024)S(1)} %get-tuple-element.4), channel_id=1, replica_groups=mesh['dp'=4,'mp'=8] {'dp','mp'}, use_global_device_ids=true, to_apply=%region_8.0 | all-reduce | flops 6144 | bytes 49152 | tf_op jit(solution)/shard_map/psum | solution.py:46
  242.2 0.6 broadcast_multiply_fusion
  242.8 1.8 fusion.17
  (3 shorter events, 0.0 us)
Async XLA Ops:
  7.2 30.3 %all-gather.7.cloned.1.call-start = ((), (), s32[]{:S(2)}) async-start(), calls=%async_computation.4 | async-start | bytes 1769472 | tf_op jit(solution)/shard_map/all_gather | solution.py:26
  11.2 52.3 %all-gather.5.cloned.1.call-start = ((), (), s32[]{:S(2)}) async-start(), calls=%async_computation.3 | async-start | bytes 1769472 | tf_op jit(solution)/shard_map/all_gather | solution.py:27
  12.0 117.7 %all-gather.11.cloned.1.call-start = ((), (), s32[]{:S(2)}) async-start(), calls=%async_computation.7 | async-start | bytes 2621440 | tf_op jit(solution)/shard_map/all_gather | solution.py:58
  50.6 108.7 %all-gather.9.cloned.1.call-start = ((), (), s32[]{:S(2)}) async-start(), calls=%async_computation.6 | async-start | bytes 2621440 | tf_op jit(solution)/shard_map/all_gather | solution.py:59
  77.8 14.5 %copy-start = (bf16[128,6144]{1,0:T(8,128)(2,1)S(1)}, bf16[128,6144]{1,0:T(8,128)(2,1)}, u32[]{:S(2)}) copy-start(bf16[128,6144]{1,0:T(8,128)(2,1)} %all-gather.5.cloned.1.call-done) | copy-start | bytes 4718596
  77.9 118.6 %reduce-scatter.2.cloned.1.call-start = ((), (), s32[]{:S(2)}) async-start(), calls=%async_computation.5 | async-start | bytes 3538944 | tf_op jit(solution)/shard_map/reduce_scatter | solution.py:35
  92.4 8.4 %copy-start.1 = (bf16[128,6144]{1,0:T(8,128)(2,1)S(1)}, bf16[128,6144]{1,0:T(8,128)(2,1)}, u32[]{:S(2)}) copy-start(bf16[128,6144]{1,0:T(8,128)(2,1)} %all-gather.7.cloned.1.call-done) | copy-start | bytes 4718596
  96.5 29.0 %all-to-all-start.1 = ((bf16[128,4,1536]{2,0,1:T(8,128)(2,1)}), bf16[128,4,1536]{2,0,1:T(8,128)(2,1)S(1)}, u32[]{:S(2)}, u32[]{:S(2)}) async-start(bf16[128,4,1536]{2,0,1:T(8,128)(2,1)} %copy.17), calls=%async_computation.2 | async-start | bytes 3145728 | tf_op jit(solution)/shard_map/all_to_all | solution.py:55
  125.6 33.7 %all-to-all-start = ((bf16[128,4,1536]{0,2,1:T(8,128)(2,1)}), bf16[128,4,1536]{0,2,1:T(8,128)(2,1)S(1)}, u32[]{:S(2)}, u32[]{:S(2)}) async-start(bf16[128,4,1536]{0,2,1:T(8,128)(2,1)} %bitcast), calls=%async_computation.1 | async-start | bytes 3145728 | tf_op jit(solution)/shard_map/all_to_all | solution.py:54
  182.4 14.0 %copy-start.2 = (bf16[16,6144]{1,0:T(8,128)(2,1)S(1)}, bf16[16,6144]{1,0:T(8,128)(2,1)}, u32[]{:S(2)}) copy-start(bf16[16,6144]{1,0:T(8,128)(2,1)} %param.5) | copy-start | bytes 589828
  182.4 14.0 %copy-start.3 = (f32[6144]{0:T(1024)S(1)}, f32[6144]{0:T(1024)}, u32[]{:S(2)}) copy-start(f32[6144]{0:T(1024)} %param.6) | copy-start | bytes 73732
Sparse Core Ops, SparseCore 0:
  11.4 26.0 all-gather.6
  39.1 24.3 all-gather.4
  65.4 34.6 all-gather.10
  101.8 52.6 all-gather.8
  156.6 39.8 reduce-scatter.1
where the time goes:
time: 252 us; the launch traced here: 251 us
  waiting for transfers between devices  82.5 us (33%)
  matrix products  69.9 us (28%)
  blocking collectives  44.4 us (18%)
  other arithmetic  26.2 us (10%)
  between operations  13.8 us (5%)
  starting transfers between devices  8.55 us (3%)
  local copies, waits for them, and re-layouts  5.71 us (2%)
    psum x1, blocking collectives, per_device(): lax.psum(jnp.sum(norm_grad * x_hat, axis=0), ('dp', 'mp')) * factor  44.4 us
    all_gather x1, waiting for transfers between devices, per_device(): lax.all_gather(normed, 'mp', axis=0, tiled=True)  25.4 us
    all_to_all x1, waiting for transfers between devices, per_device(): lax.all_to_all(cotan_all, 'dp', split_axis=1, concat_axis=0, tiled=True)  23.3 us
    all_to_all x1, waiting for transfers between devices, per_device(): lax.all_to_all(normed_all, 'dp', split_axis=1, concat_axis=0, tiled=True)  15.4 us
    dot_general x1, matrix products, per_device(): lax.dot_general(pre_grad, up_weight, (((1,), (1,)), ((), ())), preferred_...  14.4 us
    dot_general x1, matrix products, per_device(): lax.dot_general(cotan_all, down_weight, (((1,), (1,)), ((), ())), preferr...  14.3 us
    dot_general x1, matrix products, per_device(): jnp.einsum('rtf,rtk->rfk', stacked(hidden_all), stacked(cotan_cols), pref...  14.2 us
    dot_general x1, matrix products, per_device(): jnp.einsum('rtk,rtf->rkf', stacked(normed_cols), stacked(pre_all), prefer...  14 us
  transfers between devices with their start and end apart: 7, of which 5 were waited for; matrix products, arithmetic and copies ran while one was open for 37% of the time, Pallas kernels for 0%

commit v1 on v0

--- a/solution.py
+++ b/solution.py
@@ -3,6 +3,27 @@
 import jax.numpy as jnp
 from jax import lax
 from jax.sharding import PartitionSpec as P
+
+
+def collect(array, axis, dim):
+    peers, place, width = (lax.axis_size(axis), lax.axis_index(axis), array.shape[dim])
+    right = [(i, (i + 1) % peers) for i in range(peers)]
+    backward = [(i, (i - 1) % peers) for i in range(peers)]
+    filled = jnp.zeros((*array.shape[:dim], peers * width, *array.shape[dim + 1 :]), array.dtype)
+    filled = lax.dynamic_update_slice_in_dim(filled, array, place * width, axis=dim)
+    from_left = from_right = array
+    half = peers // 2
+    for step in range(1, half + 1):
+        from_left = lax.ppermute(from_left, axis, right)
+        filled = lax.dynamic_update_slice_in_dim(
+            filled, from_left, (place - step) % peers * width, axis=dim
+        )
+        if step < peers - half:
+            from_right = lax.ppermute(from_right, axis, backward)
+            filled = lax.dynamic_update_slice_in_dim(
+                filled, from_right, (place + step) % peers * width, axis=dim
+            )
+    return filled
 
 
 def gelu_value(preact):
@@ -23,7 +44,7 @@
     x_hat = centered * inv_std
     normed = (x_hat * norm_gain).astype(jnp.bfloat16)
     normed_all, cotan_all = (
-        lax.all_gather(normed, "mp", axis=0, tiled=True),
+        collect(normed, "mp", 0),
         lax.all_gather(out_grad, "mp", axis=0, tiled=True),
     )
     preact = jnp.dot(normed_all, up_weight, preferred_element_type=jnp.float32)

time: 252 us -> 380 us (1.51)
  local copies, waits for them, and re-layouts: 5.71 us -> 138 us
  waiting for transfers between devices: 82.5 us -> 44.6 us
  blocking collectives: 44.4 us -> 73.3 us
  starting transfers between devices: 8.55 us -> 12.4 us
    dynamic_update_slice x0 -> x8, local copies, waits for them, and re-layouts: none -> 127 us  [the longest x4 62.4 us: collect(): lax.dynamic_update_slice_in_dim(filled, from_left, (place - step) % peers...]
    all_to_all x0 -> x1, blocking collectives: none -> 28.7 us  [per_device(): lax.all_to_all(cotan_all, 'dp', split_axis=1, concat_axis=0, tiled=True)]
    all_gather x1 -> x0, waiting for transfers between devices: 25.4 us -> none  [per_device(): lax.all_gather(normed, 'mp', axis=0, tiled=True)]
    all_to_all x1 -> x0, waiting for transfers between devices: 23.3 us -> none  [per_device(): lax.all_to_all(cotan_all, 'dp', split_axis=1, concat_axis=0, tiled=True)]
    ppermute x0 -> x7, waiting for transfers between devices: none -> 18 us  [the longest x3 13.4 us: collect(): from_right = lax.ppermute(from_right, axis, backward)]
    reduce_scatter x1, waiting for transfers between devices: 4.71 us -> 18.9 us  [per_device(): lax.psum_scatter(lax.dot_general(pre_grad, up_weight, (((1,), (1,)), ((),...]
    all_gather x1, waiting for transfers between devices: 12.9 us -> 0.02 us  [per_device(): lax.all_gather(out_grad, 'mp', axis=0, tiled=True)]
    all_to_all x1, waiting for transfers between devices: 15.4 us -> 7.43 us  [per_device(): lax.all_to_all(normed_all, 'dp', split_axis=1, concat_axis=0, tiled=True)]
  transfers between devices with their start and end apart: 7 -> 12, of which waited for: 5 -> 7; matrix products, arithmetic and copies ran while one was open for 37% -> 60% of each run, Pallas kernels for 0% -> 0%
where the time goes in v1:
time: 380 us; the launch traced here: 378 us
  local copies, waits for them, and re-layouts  138 us (36%)
  blocking collectives  73.3 us (19%)
  matrix products  69.9 us (18%)
  waiting for transfers between devices  44.6 us (12%)
  other arithmetic  25.4 us (7%)
  between operations  13.9 us (4%)
  starting transfers between devices  12.4 us (3%)
    dynamic_update_slice x4, local copies, waits for them, and re-layouts, collect(): lax.dynamic_update_slice_in_dim(filled, from_left, (place - step) % peers...  62.4 us
    dynamic_update_slice x3, local copies, waits for them, and re-layouts, collect(): lax.dynamic_update_slice_in_dim(filled, from_right, (place + step) % peer...  48.7 us
    psum x1, blocking collectives, per_device(): lax.psum(jnp.sum(norm_grad * x_hat, axis=0), ('dp', 'mp')) * factor  44.6 us
    all_to_all x1, blocking collectives, per_device(): lax.all_to_all(cotan_all, 'dp', split_axis=1, concat_axis=0, tiled=True)  28.7 us
    reduce_scatter x1, waiting for transfers between devices, per_device(): lax.psum_scatter(lax.dot_general(pre_grad, up_weight, (((1,), (1,)), ((),...  18.9 us
    dynamic_update_slice x1, local copies, waits for them, and re-layouts, collect(): lax.dynamic_update_slice_in_dim(filled, array, place * width, axis=dim)  16.2 us
    dot_general x1, matrix products, per_device(): lax.dot_general(pre_grad, up_weight, (((1,), (1,)), ((), ())), preferred_...  14.4 us
    dot_general x1, matrix products, per_device(): lax.dot_general(cotan_all, down_weight, (((1,), (1,)), ((), ())), preferr...  14.3 us
  transfers between devices with their start and end apart: 12, of which 7 were waited for; matrix products, arithmetic and copies ran while one was open for 60% of the time, Pallas kernels for 0%

profile of v1, /device:TPU:10, one launch (start us, length us, event | category | flops | bytes accessed | tf_op | source)
XLA Modules:
  0.0 377.5 jit_solution(7640775667031258969)
XLA Ops:
  7.2 1.1 convert_reduce_fusion.2
  8.3 1.2 fusion.19
  9.5 1.1 fusion.13
  10.5 0.1 collective-permute-start
  10.7 1.8 collective-permute-start.1
  12.5 3.2 collective-permute-done
  15.7 1.9 collective-permute-done.1
  17.6 1.9 collective-permute-start.3
  19.5 1.3 collective-permute-done.2
  20.8 11.6 %collective-permute-done.3 = bf16[16,6144]{1,0:T(8,128)(2,1)S(1)} collective-permute-done((bf16[16,6144]{1,0:T(8,128)(2,1)S(1)}, bf16[16,6144]{1,0:T(8,128)(2,1)S(1)}, u32[]{:S(2)}, u32[]{:S(2)}) %collective-permute-start.3) | collective-permute-done | bytes 196640 | tf_op jit(solution)/shard_map/ppermute | solution.py:22
  32.4 4.2 %collective-permute-start.5 = (bf16[16,6144]{1,0:T(8,128)(2,1)S(1)}, bf16[16,6144]{1,0:T(8,128)(2,1)S(1)}, u32[]{:S(2)}, u32[]{:S(2)}) collective-permute-start(bf16[16,6144]{1,0:T(8,128)(2,1)S(1)} %collective-permute-done.3), channel_id=1, source_target_pairs={{0,7},{1,0},{2,1},{3,2},{4,3},{5,4},{6,5},{7,6},{8,15},{9,8},{10,9... | collective-permute-start | bytes 589832 | tf_op jit(solution)/shard_map/ppermute | solution.py:22
  36.6 0.8 copy.31
  37.4 1.3 broadcast_in_dim.2
  38.8 16.2 %dynamic_update_slice.24 = bf16[128,6144]{0,1:T(8,128)(2,1)} dynamic-update-slice(bf16[128,6144]{0,1:T(8,128)(2,1)} %broadcast_in_dim.2, bf16[16,6144]{0,1:T(8,128)(2,1)S(1)} %copy.31, s32[]{:T(128)S(6)} %select_n.55, s32[]{:T(128)} %constant.70.clone.1) | dynamic-update-slice | bytes 393220 | tf_op jit(solution)/shard_map/dynamic_update_slice | solution.py:13
  55.0 0.8 copy.32
  55.8 16.2 %dynamic_update_slice.25 = bf16[128,6144]{0,1:T(8,128)(2,1)} dynamic-update-slice(bf16[128,6144]{0,1:T(8,128)(2,1)} %dynamic_update_slice.24, bf16[16,6144]{0,1:T(8,128)(2,1)S(1)} %copy.32, s32[]{:T(128)S(6)} %select_n.57, s32[]{:T(128)} %constant.70.clone.1) | dynamic-update-slice | bytes 393220 | tf_op jit(solution)/shard_map/dynamic_update_slice | solution.py:18
  72.0 0.8 copy.33
  72.8 16.2 %dynamic_update_slice.26 = bf16[128,6144]{0,1:T(8,128)(2,1)} dynamic-update-slice(bf16[128,6144]{0,1:T(8,128)(2,1)} %dynamic_update_slice.25, bf16[16,6144]{0,1:T(8,128)(2,1)S(1)} %copy.33, s32[]{:T(128)S(6)} %select_n.59, s32[]{:T(128)} %constant.70.clone.1) | dynamic-update-slice | bytes 393220 | tf_op jit(solution)/shard_map/dynamic_update_slice | solution.py:23
  89.1 0.8 copy.34
  89.9 13.7 %dynamic_update_slice.27 = bf16[128,6144]{0,1:T(8,128)(2,1)} dynamic-update-slice(bf16[128,6144]{0,1:T(8,128)(2,1)} %dynamic_update_slice.26, bf16[16,6144]{0,1:T(8,128)(2,1)S(1)} %copy.34, s32[]{:T(128)S(6)} %select_n.61, s32[]{:T(128)} %constant.70.clone.1) | dynamic-update-slice | bytes 393220 | tf_op jit(solution)/shard_map/dynamic_update_slice | solution.py:18
  103.6 0.8 copy.35
  104.4 16.2 %dynamic_update_slice.28 = bf16[128,6144]{0,1:T(8,128)(2,1)} dynamic-update-slice(bf16[128,6144]{0,1:T(8,128)(2,1)} %dynamic_update_slice.27, bf16[16,6144]{0,1:T(8,128)(2,1)S(1)} %copy.35, s32[]{:T(128)S(6)} %select_n.63, s32[]{:T(128)} %constant.70.clone.1) | dynamic-update-slice | bytes 393220 | tf_op jit(solution)/shard_map/dynamic_update_slice | solution.py:23
  120.6 0.8 copy.36
  121.4 16.2 %dynamic_update_slice.29 = bf16[128,6144]{0,1:T(8,128)(2,1)} dynamic-update-slice(bf16[128,6144]{0,1:T(8,128)(2,1)} %dynamic_update_slice.28, bf16[16,6144]{0,1:T(8,128)(2,1)S(1)} %copy.36, s32[]{:T(128)S(6)} %select_n.65, s32[]{:T(128)} %constant.70.clone.1) | dynamic-update-slice | bytes 393220 | tf_op jit(solution)/shard_map/dynamic_update_slice | solution.py:18
  137.7 0.8 copy.37
  138.5 16.2 %dynamic_update_slice.30 = bf16[128,6144]{0,1:T(8,128)(2,1)} dynamic-update-slice(bf16[128,6144]{0,1:T(8,128)(2,1)} %dynamic_update_slice.29, bf16[16,6144]{0,1:T(8,128)(2,1)S(1)} %copy.37, s32[]{:T(128)S(6)} %select_n.67, s32[]{:T(128)} %constant.70.clone.1) | dynamic-update-slice | bytes 393220 | tf_op jit(solution)/shard_map/dynamic_update_slice | solution.py:23
  154.7 0.8 copy.38
  155.5 16.2 %dynamic_update_slice.31 = bf16[128,6144]{0,1:T(8,128)(2,1)} dynamic-update-slice(bf16[128,6144]{0,1:T(8,128)(2,1)} %dynamic_update_slice.30, bf16[16,6144]{0,1:T(8,128)(2,1)S(1)} %copy.38, s32[]{:T(128)S(6)} %select_n.69, s32[]{:T(128)} %constant.70.clone.1) | dynamic-update-slice | bytes 393220 | tf_op jit(solution)/shard_map/dynamic_update_slice | solution.py:18
  171.7 12.9 %multiply_convert_fusion.2 = (bf16[128,2048]{1,0:T(8,128)(2,1)}, f32[128,2048]{1,0:T(8,128)S(1)}) fusion(bf16[128,6144]{0,1:T(8,128)(2,1)} %dynamic_update_slice.31, bf16[6144,2048]{1,0:T(8,128)(2,1)} %param.7), kind=kOutput, calls=%fused_computation.15 | convolution fusion | flops 3222536192 | bytes 28311552 | tf_op jit(solution)/shard_map/dot_general | solution.py:50
  184.7 0.2 all-gather.6.cloned.1.call-start
  185.0 14.3 %fusion = bf16[128,2048]{1,0:T(8,128)(2,1)} fusion(bf16[128,6144]{1,0:T(8,128)(2,1)} %all-gather.4.cloned.1.call-done, bf16[2048,6144]{1,0:T(8,128)(2,1)} %param.8, f32[128,2048]{1,0:T(8,128)S(1)} %get-tuple-element.8), kind=kOutput, calls=%fused_computation.7 | convolution fusion | flops 3223846912 | bytes 28311552 | tf_op jit(solution)/shard_map/dot_general | solution.py:52
  199.3 14.4 %fusion.20 = f32[128,6144]{1,0:T(8,128)} fusion(bf16[128,2048]{1,0:T(8,128)(2,1)} %fusion, bf16[6144,2048]{1,0:T(8,128)(2,1)} %param.7), kind=kOutput, calls=%fused_computation.38 | convolution fusion | flops 3221225472 | bytes 28835840 | tf_op jit(solution)/shard_map/dot_general | solution.py:57
  213.8 1.4 copy-done
  215.1 0.9 copy.40
  216.0 0.7 copy.41
  216.8 28.7 %all_to_all.32 = bf16[128,4,1536]{2,0,1:T(8,128)(2,1)S(1)} all-to-all(bf16[128,4,1536]{2,0,1:T(8,128)(2,1)S(1)} %copy.41), channel_id=1, replica_groups=mesh['dp'=4,'mp'=8] {'dp'}, dimensions={1} | all-to-all | bytes 3145728 | tf_op jit(solution)/shard_map/all_to_all | solution.py:76
  245.5 4.1 %all-to-all-start = ((bf16[128,4,1536]{0,2,1:T(8,128)(2,1)}), bf16[128,4,1536]{0,2,1:T(8,128)(2,1)S(1)}, u32[]{:S(2)}, u32[]{:S(2)}) async-start(bf16[128,4,1536]{0,2,1:T(8,128)(2,1)} %bitcast), calls=%async_computation.1 | async-start | bytes 3145728 | tf_op jit(solution)/shard_map/all_to_all | solution.py:75
  249.6 14.2 %convert_reduce_fusion = f32[2048,1536]{1,0:T(8,128)} fusion(bf16[4,128,2048]{2,1,0:T(8,128)(2,1)} %bitcast.19, bf16[128,4,1536]{2,0,1:T(8,128)(2,1)S(1)} %all_to_all.32), kind=kOutput, calls=%fused_computation | convolution fusion | flops 3255828480 | bytes 16252928 | tf_op jit(solution)/shard_map/rtf,rtk->rfk/dot_general | solution.py:89
  263.8 9.0 %multiply_convert_fusion = bf16[2048,1536]{1,0:T(8,128)(2,1)} fusion(f32[2048,1536]{1,0:T(8,128)} %convert_reduce_fusion), kind=kLoop, calls=%fused_computation.4 | loop fusion | flops 6291456 | bytes 18874368 | tf_op jit(solution)/shard_map/convert_element_type | solution.py:95
  272.8 7.4 %all-to-all-done = bf16[128,4,1536]{0,2,1:T(8,128)(2,1)S(1)} async-done(((bf16[128,4,1536]{0,2,1:T(8,128)(2,1)}), bf16[128,4,1536]{0,2,1:T(8,128)(2,1)S(1)}, u32[]{:S(2)}, u32[]{:S(2)}) %all-to-all-start) | async-done | bytes 1572896 | tf_op jit(solution)/shard_map/all_to_all | solution.py:75
  280.2 0.2 all-gather.6.cloned.1.call-done
  280.4 14.1 %convert_reduce_fusion.1 = f32[1536,2048]{1,0:T(8,128)} fusion(bf16[4,128,2048]{2,1,0:T(8,128)(2,1)} %bitcast.20, bf16[128,4,1536]{0,2,1:T(8,128)(2,1)S(1)} %all-to-all-done), kind=kOutput, calls=%fused_computation.1 | convolution fusion | flops 3255828480 | bytes 16252928 | tf_op jit(solution)/shard_map/rtk,rtf->rkf/dot_general | solution.py:86
  294.5 9.3 %multiply_convert_fusion.1 = bf16[1536,2048]{1,0:T(8,128)(2,1)} fusion(f32[1536,2048]{1,0:T(8,128)} %convert_reduce_fusion.1), kind=kLoop, calls=%fused_computation.5 | loop fusion | flops 6291456 | bytes 18874368 | tf_op jit(solution)/shard_map/convert_element_type | solution.py:94
  303.7 18.9 %reduce-scatter.2.cloned.1.call-done = f32[16,6144]{1,0:T(8,128)} async-done(((f32[128,6144]{1,0:T(8,128)}), f32[16,6144]{1,0:T(8,128)}) %reduce-scatter.2.cloned.1.call-update) | async-done | bytes 393232 | tf_op jit(solution)/shard_map/reduce_scatter | solution.py:56
  322.6 1.3 fusion.18
  323.9 44.6 %psum.7 = f32[6144]{0:T(1024)S(1)} all-reduce(f32[6144]{0:T(1024)S(1)} %get-tuple-element.4), channel_id=1, replica_groups=mesh['dp'=4,'mp'=8] {'dp','mp'}, use_global_device_ids=true, to_apply=%region_8.9 | all-reduce | flops 6144 | bytes 49152 | tf_op jit(solution)/shard_map/psum | solution.py:67
  368.5 0.6 broadcast_multiply_fusion
  369.1 1.8 fusion.17
  (23 shorter events, 0.2 us)
Async XLA Ops:
  7.2 177.8 %all-gather.4.cloned.1.call-start = ((), (), s32[]{:S(2)}) async-start(), calls=%async_computation.3 | async-start | bytes 1769472 | tf_op jit(solution)/shard_map/all_gather | solution.py:48
  10.5 5.1 %collective-permute-start = (bf16[16,6144]{1,0:T(8,128)(2,1)S(1)}, bf16[16,6144]{1,0:T(8,128)(2,1)S(1)}, u32[]{:S(2)}, u32[]{:S(2)}) collective-permute-start(bf16[16,6144]{1,0:T(8,128)(2,1)S(1)} %fusion.13), channel_id=1, source_target_pairs={{0,1},{1,2},{2,3},{3,4},{4,5},{5,6},{6,7},{7,0},{8,9},{9,10},{10,1... | collective-permute-start | bytes 589832 | tf_op jit(solution)/shard_map/ppermute | solution.py:17
  10.6 239.0 %all-gather.8.cloned.1.call-start = ((), (), s32[]{:S(2)}) async-start(), calls=%async_computation.6 | async-start | bytes 2621440 | tf_op jit(solution)/shard_map/all_gather | solution.py:79
  10.7 6.9 %collective-permute-start.1 = (bf16[16,6144]{1,0:T(8,128)(2,1)S(1)}, bf16[16,6144]{1,0:T(8,128)(2,1)S(1)}, u32[]{:S(2)}, u32[]{:S(2)}) collective-permute-start(bf16[16,6144]{1,0:T(8,128)(2,1)S(1)} %fusion.13), channel_id=1, source_target_pairs={{0,7},{1,0},{2,1},{3,2},{4,3},{5,4},{6,5},{7,6},{8,15},{9,8},{10,9... | collective-permute-start | bytes 589832 | tf_op jit(solution)/shard_map/ppermute | solution.py:22
  15.7 5.1 %collective-permute-start.2 = (bf16[16,6144]{1,0:T(8,128)(2,1)S(1)}, bf16[16,6144]{1,0:T(8,128)(2,1)S(1)}, u32[]{:S(2)}, u32[]{:S(2)}) collective-permute-start(bf16[16,6144]{1,0:T(8,128)(2,1)S(1)} %collective-permute-done), channel_id=1, source_target_pairs={{0,1},{1,2},{2,3},{3,4},{4,5},{5,6},{6,7},{7,0},{8,9},{9,10},{10,1... | collective-permute-start | bytes 589832 | tf_op jit(solution)/shard_map/ppermute | solution.py:17
  17.6 14.8 %collective-permute-start.3 = (bf16[16,6144]{1,0:T(8,128)(2,1)S(1)}, bf16[16,6144]{1,0:T(8,128)(2,1)S(1)}, u32[]{:S(2)}, u32[]{:S(2)}) collective-permute-start(bf16[16,6144]{1,0:T(8,128)(2,1)S(1)} %collective-permute-done.1), channel_id=1, source_target_pairs={{0,7},{1,0},{2,1},{3,2},{4,3},{5,4},{6,5},{7,6},{8,15},{9,8},{10,9... | collective-permute-start | bytes 589832 | tf_op jit(solution)/shard_map/ppermute | solution.py:22
  20.8 15.8 %collective-permute-start.4 = (bf16[16,6144]{1,0:T(8,128)(2,1)S(1)}, bf16[16,6144]{1,0:T(8,128)(2,1)S(1)}, u32[]{:S(2)}, u32[]{:S(2)}) collective-permute-start(bf16[16,6144]{1,0:T(8,128)(2,1)S(1)} %collective-permute-done.2), channel_id=1, source_target_pairs={{0,1},{1,2},{2,3},{3,4},{4,5},{5,6},{6,7},{7,0},{8,9},{9,10},{10,1... | collective-permute-start | bytes 589832 | tf_op jit(solution)/shard_map/ppermute | solution.py:17
  32.4 105.3 %collective-permute-start.5 = (bf16[16,6144]{1,0:T(8,128)(2,1)S(1)}, bf16[16,6144]{1,0:T(8,128)(2,1)S(1)}, u32[]{:S(2)}, u32[]{:S(2)}) collective-permute-start(bf16[16,6144]{1,0:T(8,128)(2,1)S(1)} %collective-permute-done.3), channel_id=1, source_target_pairs={{0,7},{1,0},{2,1},{3,2},{4,3},{5,4},{6,5},{7,6},{8,15},{9,8},{10,9... | collective-permute-start | bytes 589832 | tf_op jit(solution)/shard_map/ppermute | solution.py:22
  36.6 118.1 %collective-permute-start.6 = (bf16[16,6144]{1,0:T(8,128)(2,1)S(1)}, bf16[16,6144]{1,0:T(8,128)(2,1)S(1)}, u32[]{:S(2)}, u32[]{:S(2)}) collective-permute-start(bf16[16,6144]{1,0:T(8,128)(2,1)S(1)} %collective-permute-done.4), channel_id=1, source_target_pairs={{0,1},{1,2},{2,3},{3,4},{4,5},{5,6},{6,7},{7,0},{8,9},{9,10},{10,1... | collective-permute-start | bytes 589832 | tf_op jit(solution)/shard_map/ppermute | solution.py:17
  184.7 95.7 %all-gather.6.cloned.1.call-start = ((), (), s32[]{:S(2)}) async-start(), calls=%async_computation.5 | async-start | bytes 2621440 | tf_op jit(solution)/shard_map/all_gather | solution.py:80
  199.3 123.4 %reduce-scatter.2.cloned.1.call-start = ((), (), s32[]{:S(2)}) async-start(), calls=%async_computation.4 | async-start | bytes 3538944 | tf_op jit(solution)/shard_map/reduce_scatter | solution.py:56
  213.7 1.4 copy-start
  245.5 34.7 %all-to-all-start = ((bf16[128,4,1536]{0,2,1:T(8,128)(2,1)}), bf16[128,4,1536]{0,2,1:T(8,128)(2,1)S(1)}, u32[]{:S(2)}, u32[]{:S(2)}) async-start(bf16[128,4,1536]{0,2,1:T(8,128)(2,1)} %bitcast), calls=%async_computation.1 | async-start | bytes 3145728 | tf_op jit(solution)/shard_map/all_to_all | solution.py:75
  294.4 28.2 %copy-start.1 = (bf16[16,6144]{1,0:T(8,128)(2,1)S(1)}, bf16[16,6144]{1,0:T(8,128)(2,1)}, u32[]{:S(2)}) copy-start(bf16[16,6144]{1,0:T(8,128)(2,1)} %param.5) | copy-start | bytes 589828
  294.4 28.2 %copy-start.2 = (f32[6144]{0:T(1024)S(1)}, f32[6144]{0:T(1024)}, u32[]{:S(2)}) copy-start(f32[6144]{0:T(1024)} %param.6) | copy-start | bytes 73732
Sparse Core Ops, SparseCore 0:
  10.8 32.6 all-gather.3
  184.8 44.2 all-gather.7
  231.0 49.3 all-gather.5
  282.5 40.0 reduce-scatter.1
